TPU v7x, 1024 devices: a whole 4x4x32 slice. The times are simulated.
1024 devices in a mesh: cells: 128 (over y, z), orb: 8 (over x, core).
Axes of the slice: x: 4, y: 4, z: 32, core: 2. Of those that a mesh axis runs over, the one named last changes fastest.
Arguments:
- initial: float32 [512, 65536], P('orb', 'cells'), may hold values from -500 to 500, as said below
- cell_matrices: float32 [128, 512, 512], P('cells'), may hold values from -0.22097087 to 0.22097087, as said below
- cell_map: int32 [128, 512], P('cells'), may hold values from 0 to 511, as said below
- face_low: int32 [128, 64], P('cells'), may hold values from 0 to 511, as said below
- face_high: int32 [128, 64], P('cells'), may hold values from 0 to 511, as said below
Outputs:
- orbitals: float32 [512, 65536], P('orb', 'cells')
Inputs may be any that keep to these rules, and one draw needn't show every extreme that they name: `cell_map`: row c holds the device-local numbers of cell c's 512 nodes in the order of cell_matrices' rows; within the 1 cells of one device every number is used, a node belongs to one or two of them. `face_low`: distinct numbers, each in exactly one cell of the device, none also in face_high of the same device; entry k names the same physical node as entry k of face_high of the previous device along the periodic chain. `face_high`: distinct numbers, each in exactly one cell of the device; entry k names the same physical node as entry k of face_low of the next device along the periodic chain. `cell_matrices`: each cell's matrix is symmetric. `initial`: copies of a shared node may differ; only the face_high copy counts.
All inputs are finite; a program needn't handle non-finite values. Where the computation divides by a largest or mean magnitude, that divisor is 1e-20 or more.
Results may differ from a plain program's by a relative error of at most 0.0003.
Values sent between devices are 32-bit elements; how exact they have to be, the bound alone decides.
A program may use at most 32 MiB of HBM per device.

v0:
```python
import jax
import jax.numpy as jnp
from jax import lax
from jax.sharding import PartitionSpec as P

DEGREE = 7
NS_ITERS = 3


center_value = 0.6
half_width = 1.6
highest = lax.Precision.HIGHEST


def with_halo(block, sides, width):
    for axis, dim in sides:
        count = lax.axis_size(axis)
        forward = [(i, i + 1) for i in range(count - 1)]
        forward.append((count - 1, 0))
        backward = [(target, source) for source, target in forward]
        low = lax.ppermute(
            lax.slice_in_dim(block, block.shape[dim] - width, None, axis=dim), axis, forward
        )
        high = lax.ppermute(lax.slice_in_dim(block, 0, width, axis=dim), axis, backward)
        block = jnp.concatenate([low, block, high], axis=dim)
    return block


def assemble(values, face_low, face_high):
    lower_index = face_low[0]
    upper_index = face_high[0]
    rims = jnp.stack([values[:, lower_index], values[:, upper_index]])
    padded = with_halo(rims, (("cells", 0),), 1)
    values = values.at[:, lower_index].add(padded[0])
    return values.at[:, upper_index].add(padded[3])


def apply_operator(values, matrices, cell_map, face_low, face_high):
    gathered = values[:, cell_map]
    product = jnp.einsum("ocn,cmn->ocm", gathered, matrices, precision=highest)
    summed = jnp.zeros_like(values).at[:, cell_map].add(product)
    return assemble(summed, face_low, face_high)


def chebyshev(values, matrices, cell_map, face_low, face_high):
    previous = values
    current = (
        apply_operator(values, matrices, cell_map, face_low, face_high) - center_value * values
    ) / half_width
    for degree_index in range(DEGREE - 1):
        image = apply_operator(current, matrices, cell_map, face_low, face_high)
        following = 2.0 * (image - center_value * current) / half_width - previous
        previous, current = (current, following)
    return current


def inverse_root(correlation, first, width):
    dscale = 1.0 / jnp.sqrt(jnp.diagonal(correlation))
    scaled = correlation * dscale[:, None] * dscale[None, :]
    bound_scale = jnp.max(jnp.sum(jnp.abs(scaled), axis=1))
    target = scaled / bound_scale
    identity = jnp.eye(correlation.shape[0], dtype=jnp.float32)
    root_factor = 0.5 * (3.0 * identity - target)
    columns = lax.dynamic_slice_in_dim(root_factor, first, width, 1)
    for iteration in range(NS_ITERS - 1):
        columns = lax.dynamic_slice_in_dim(root_factor, first, width, 1)
        inner_term = jnp.dot(root_factor, columns, precision=highest)
        inner_term = jnp.dot(target, inner_term, precision=highest)
        inner_term = jnp.dot(root_factor, inner_term, precision=highest)
        columns = 0.5 * (3.0 * columns - inner_term)
        if iteration + 1 < NS_ITERS - 1:
            root_factor = lax.all_gather(columns, "orb", axis=1, tiled=True)
    return (dscale, bound_scale, columns)


def body(initial, cell_matrices, cell_map, face_low, face_high):
    width = initial.shape[0]
    local_nodes = initial.shape[1]
    first = lax.axis_index("orb") * width
    owned = jnp.ones((local_nodes,), jnp.float32).at[face_low[0]].set(0.0)
    owned_count = lax.axis_size("cells") * (local_nodes - face_low.shape[1])
    orbitals = assemble(initial * owned[None, :], face_low, face_high)
    orbitals = chebyshev(orbitals, cell_matrices, cell_map, face_low, face_high)
    everything = lax.all_gather(orbitals, "orb", axis=0, tiled=True)
    local_terms = jnp.dot(everything * owned[None, :], orbitals.T, precision=highest)
    column_block = lax.psum(local_terms, "cells") / owned_count
    correlation = lax.all_gather(column_block, "orb", axis=1, tiled=True)
    dscale, bound_scale, columns = inverse_root(correlation, first, width)
    mixing = dscale[:, None] * columns / jnp.sqrt(bound_scale)
    orbitals = jnp.dot(mixing.T, everything, precision=highest)
    return orbitals


def solution(mesh):
    placed = (
        P("orb", "cells"),
        P("cells", None, None),
        P("cells", None),
        P("cells", None),
        P("cells", None),
    )
    return jax.shard_map(
        body, mesh=mesh, in_specs=placed, out_specs=P("orb", "cells"), check_vma=False
    )
```

profile of v0, /device:TPU:1, one launch (start us, length us, event | category | flops | bytes accessed | tf_op | source)
XLA Modules:
  0.0 800.9 jit_solution(7317545385917343297)
XLA Ops:
  9.9 4.4 collective-permute-start
  14.9 19.2 %collective-permute-start.1 = (f32[1,64,64]{1,2,0:T(8,128)S(1)}, f32[1,64,64]{1,2,0:T(8,128)S(1)}, u32[]{:S(2)}, u32[]{:S(2)}) collective-permute-start(f32[1,64,64]{1,2,0:T(8,128)S(1)} %bitcast.193), channel_id=1, source_target_pairs={{8,0},{16,8},{24,16},{32,24},{40,32},{48,40},{56,48},{64,56},{72,6... | collective-permute-start | bytes 49160 | tf_op jit(solution)/shard_map/ppermute | solution.py:24
  38.6 2.3 scatter_custom_fusion.3
  44.0 6.9 collective-permute-start.3
  55.4 2.3 scatter_custom_fusion.6
  58.9 1.9 collective-permute-start.4
  60.9 6.9 collective-permute-start.5
  72.4 2.3 scatter_custom_fusion.9
  77.9 6.9 collective-permute-start.7
  89.3 2.3 scatter_custom_fusion.12
  94.7 6.9 collective-permute-start.9
  106.1 2.3 scatter_custom_fusion.15
  111.6 6.9 collective-permute-start.11
  123.2 2.3 scatter_custom_fusion.18
  128.6 6.9 collective-permute-start.13
  140.0 2.3 scatter_custom_fusion.21
  145.5 6.9 collective-permute-start.15
  155.4 34.0 %all-gather.4.cloned.1.call-done = f32[512,512]{1,0:T(8,128)} async-done(((f32[64,512]{1,0:T(8,128)}), f32[512,512]{1,0:T(8,128)}) %all-gather.4.cloned.1.call-update) | async-done | bytes 1048592 | tf_op jit(solution)/shard_map/all_gather | solution.py:84
  189.4 3.0 fusion.10
  192.6 484.7 %all-reduce.2.cloned.1.call-done = f32[512,64]{0,1:T(8,128)} async-done(((f32[512,64]{0,1:T(8,128)}), f32[512,64]{0,1:T(8,128)}) %all-reduce.2.cloned.1.call-update) | async-done | bytes 131088 | tf_op jit(solution)/shard_map/psum | solution.py:86
  679.2 53.1 %all-gather.6.cloned.1.call-done = f32[512,512]{0,1:T(8,128)} async-done(((f32[512,64]{0,1:T(8,128)}), f32[512,512]{0,1:T(8,128)}) %all-gather.6.cloned.1.call-update) | async-done | bytes 1048592 | tf_op jit(solution)/shard_map/all_gather | solution.py:87
  732.3 8.5 %gather_fusion.23 = f32[512]{0:T(512)S(1)} fusion(f32[512,512]{0,1:T(8,128)} %all-gather.6.cloned.1.call-done, s32[512]{0:T(512)S(1)} %bitcast.185), kind=kCustom, calls=%fused_computation.23 | custom fusion | bytes 8192 | tf_op jit(solution)/shard_map/jit(diagonal)/cond/branch_0_fun/gather | solution.py:58
  747.0 40.7 %all-gather.8.cloned.1.call-done = f32[512,512]{0,1:T(8,128)} async-done(((f32[512,64]{0,1:T(8,128)}), f32[512,512]{0,1:T(8,128)}) %all-gather.8.cloned.1.call-update) | async-done | bytes 1048592 | tf_op jit(solution)/shard_map/all_gather | solution.py:72
  787.7 2.0 fusion.29
  (125 shorter events, 69.9 us)
Async XLA Ops:
  6.5 30.8 %copy-start = (f32[1,512,512]{2,1,0:T(8,128)S(1)}, f32[1,512,512]{2,1,0:T(8,128)}, u32[]{:S(2)}) copy-start(f32[1,512,512]{2,1,0:T(8,128)} %param.6) | copy-start | bytes 3145732
  6.5 182.9 %all-gather.4.cloned.1.call-start = ((), (), s32[]{:S(2)}) async-start(), calls=%async_computation | async-start | bytes 1179648 | tf_op jit(solution)/shard_map/all_gather | solution.py:84
  9.9 24.3 %collective-permute-start = (f32[1,64,64]{1,2,0:T(8,128)S(1)}, f32[1,64,64]{1,2,0:T(8,128)S(1)}, u32[]{:S(2)}, u32[]{:S(2)}) collective-permute-start(f32[1,64,64]{1,2,0:T(8,128)S(1)} %bitcast.194), channel_id=1, source_target_pairs={{0,8},{8,16},{16,24},{24,32},{32,40},{40,48},{48,56},{56,64},{64,7... | collective-permute-start | bytes 49160 | tf_op jit(solution)/shard_map/ppermute | solution.py:21
  14.3 19.8 %copy-start.4 = (s32[1,512]{1,0:T(1,128)S(1)}, s32[1,512]{1,0:T(1,128)}, u32[]{:S(2)}) copy-start(s32[1,512]{1,0:T(1,128)} %param.7) | copy-start | bytes 6148
  14.9 20.3 %collective-permute-start.1 = (f32[1,64,64]{1,2,0:T(8,128)S(1)}, f32[1,64,64]{1,2,0:T(8,128)S(1)}, u32[]{:S(2)}, u32[]{:S(2)}) collective-permute-start(f32[1,64,64]{1,2,0:T(8,128)S(1)} %bitcast.193), channel_id=1, source_target_pairs={{8,0},{16,8},{24,16},{32,24},{40,32},{48,40},{56,48},{64,56},{72,6... | collective-permute-start | bytes 49160 | tf_op jit(solution)/shard_map/ppermute | solution.py:24
  42.1 8.8 %collective-permute-start.2 = (f32[1,64,64]{1,2,0:T(8,128)S(1)}, f32[1,64,64]{1,2,0:T(8,128)S(1)}, u32[]{:S(2)}, u32[]{:S(2)}) collective-permute-start(f32[1,64,64]{1,2,0:T(8,128)S(1)} %bitcast.201), channel_id=1, source_target_pairs={{0,8},{8,16},{16,24},{24,32},{32,40},{40,48},{48,56},{56,64},{64,7... | collective-permute-start | bytes 49160 | tf_op jit(solution)/shard_map/ppermute | solution.py:21
  44.0 7.9 collective-permute-start.3
  58.9 8.8 %collective-permute-start.4 = (f32[1,64,64]{1,2,0:T(8,128)S(1)}, f32[1,64,64]{1,2,0:T(8,128)S(1)}, u32[]{:S(2)}, u32[]{:S(2)}) collective-permute-start(f32[1,64,64]{1,2,0:T(8,128)S(1)} %bitcast.196), channel_id=1, source_target_pairs={{0,8},{8,16},{16,24},{24,32},{32,40},{40,48},{48,56},{56,64},{64,7... | collective-permute-start | bytes 49160 | tf_op jit(solution)/shard_map/ppermute | solution.py:21
  60.9 8.0 collective-permute-start.5
  76.0 8.8 %collective-permute-start.6 = (f32[1,64,64]{1,2,0:T(8,128)S(1)}, f32[1,64,64]{1,2,0:T(8,128)S(1)}, u32[]{:S(2)}, u32[]{:S(2)}) collective-permute-start(f32[1,64,64]{1,2,0:T(8,128)S(1)} %bitcast.197), channel_id=1, source_target_pairs={{0,8},{8,16},{16,24},{24,32},{32,40},{40,48},{48,56},{56,64},{64,7... | collective-permute-start | bytes 49160 | tf_op jit(solution)/shard_map/ppermute | solution.py:21
  77.9 8.0 collective-permute-start.7
  92.8 8.8 %collective-permute-start.8 = (f32[1,64,64]{1,2,0:T(8,128)S(1)}, f32[1,64,64]{1,2,0:T(8,128)S(1)}, u32[]{:S(2)}, u32[]{:S(2)}) collective-permute-start(f32[1,64,64]{1,2,0:T(8,128)S(1)} %bitcast.198), channel_id=1, source_target_pairs={{0,8},{8,16},{16,24},{24,32},{32,40},{40,48},{48,56},{56,64},{64,7... | collective-permute-start | bytes 49160 | tf_op jit(solution)/shard_map/ppermute | solution.py:21
  94.7 8.0 collective-permute-start.9
  109.7 8.8 %collective-permute-start.10 = (f32[1,64,64]{1,2,0:T(8,128)S(1)}, f32[1,64,64]{1,2,0:T(8,128)S(1)}, u32[]{:S(2)}, u32[]{:S(2)}) collective-permute-start(f32[1,64,64]{1,2,0:T(8,128)S(1)} %bitcast.199), channel_id=1, source_target_pairs={{0,8},{8,16},{16,24},{24,32},{32,40},{40,48},{48,56},{56,64},{64,7... | collective-permute-start | bytes 49160 | tf_op jit(solution)/shard_map/ppermute | solution.py:21
  111.6 8.0 collective-permute-start.11
  126.7 8.8 %collective-permute-start.12 = (f32[1,64,64]{1,2,0:T(8,128)S(1)}, f32[1,64,64]{1,2,0:T(8,128)S(1)}, u32[]{:S(2)}, u32[]{:S(2)}) collective-permute-start(f32[1,64,64]{1,2,0:T(8,128)S(1)} %bitcast.200), channel_id=1, source_target_pairs={{0,8},{8,16},{16,24},{24,32},{32,40},{40,48},{48,56},{56,64},{64,7... | collective-permute-start | bytes 49160 | tf_op jit(solution)/shard_map/ppermute | solution.py:21
  128.6 8.0 collective-permute-start.13
  143.6 8.8 %collective-permute-start.14 = (f32[1,64,64]{1,2,0:T(8,128)S(1)}, f32[1,64,64]{1,2,0:T(8,128)S(1)}, u32[]{:S(2)}, u32[]{:S(2)}) collective-permute-start(f32[1,64,64]{1,2,0:T(8,128)S(1)} %bitcast.195), channel_id=1, source_target_pairs={{0,8},{8,16},{16,24},{24,32},{32,40},{40,48},{48,56},{56,64},{64,7... | collective-permute-start | bytes 49160 | tf_op jit(solution)/shard_map/ppermute | solution.py:21
  145.5 8.0 collective-permute-start.15
  155.3 522.0 %all-reduce.2.cloned.1.call-start = ((), (), s32[]{:S(2)}) async-start(), calls=%async_computation.1 | async-start | bytes 262144 | tf_op jit(solution)/shard_map/psum | solution.py:86
  192.5 539.8 %all-gather.6.cloned.1.call-start = ((), (), s32[]{:S(2)}) async-start(), calls=%async_computation.2 | async-start | bytes 1179648 | tf_op jit(solution)/shard_map/all_gather | solution.py:87
  678.9 108.8 %all-gather.8.cloned.1.call-start = ((), (), s32[]{:S(2)}) async-start(), calls=%async_computation.3 | async-start | bytes 1179648 | tf_op jit(solution)/shard_map/all_gather | solution.py:72
  732.3 8.5 %copy-start.1 = (f32[512,512]{0,1:T(8,128)S(1)}, f32[512,512]{0,1:T(8,128)}, u32[]{:S(2)}) copy-start(f32[512,512]{0,1:T(8,128)} %all-gather.6.cloned.1.call-done) | copy-start | bytes 3145732
  789.7 1.7 copy-start.3
  (2 other events, 2.3 us)
Sparse Core Ops, SparseCore 0:
  155.5 33.9 all-gather.3
  192.9 484.3 all-reduce.1
  680.0 52.1 all-gather.5
  746.4 41.1 all-gather.7
where the time goes:
time: 809 us; the launch traced here: 801 us
  waiting for transfers between devices  613 us (76%)
  starting transfers between devices  85.6 us (11%)
  other arithmetic  37.6 us (5%)
  local copies, waits for them, and re-layouts  29.2 us (4%)
  matrix products  20.9 us (3%)
  between operations  15 us (2%)
    psum x1, waiting for transfers between devices, body(): column_block = lax.psum(local_terms, 'cells') / owned_count  485 us
    ppermute x8, starting transfers between devices, with_halo(): lax.ppermute(lax.slice_in_dim(block, 0, width, axis=dim), axis, backward)  67.5 us
    all_gather x1, waiting for transfers between devices, body(): correlation = lax.all_gather(column_block, 'orb', axis=1, tiled=True)  53.1 us
    all_gather x1, waiting for transfers between devices, inverse_root(): root_factor = lax.all_gather(columns, 'orb', axis=1, tiled=True)  40.7 us
    all_gather x1, waiting for transfers between devices, body(): everything = lax.all_gather(orbitals, 'orb', axis=0, tiled=True)  34 us
    ppermute x8, starting transfers between devices, with_halo(): lax.ppermute(lax.slice_in_dim(block, block.shape[dim] - width, None, axis...  17.8 us
    scatter-add x7, other arithmetic, apply_operator(): summed = jnp.zeros_like(values).at[:, cell_map].add(product)  16.2 us
  transfers between devices with their start and end apart: 20, of which 4 were waited for; matrix products, arithmetic and copies ran while one was open for 1% of the time, Pallas kernels for 0%

commit v1 on v0

v1 whole, which is shorter than its diff:
```python
import jax
import jax.numpy as jnp
from jax import lax
from jax.experimental import pallas as pl
from jax.experimental.pallas import tpu as pltpu
from jax.sharding import PartitionSpec as P

DEGREE = 7
NS_ITERS = 3
NODE = 512
FACE = 64
RIM = 2 * FACE
NORB = 512
WIDTH = 64
NX, NY, NZ, NEAR = 4, 4, 32, 4
FAR = NZ // NEAR
GROUP = NY * NEAR
MESH = pl.DeviceIdType.MESH

center_value = 0.6
half_width = 1.6
f32, bf16 = jnp.float32, jnp.bfloat16


def split(a):
    hi = a.astype(bf16)
    return hi, (a - hi.astype(f32)).astype(bf16)


def dot(a, b):
    return jnp.dot(a, b, preferred_element_type=f32)


def dot_t(a, b):
    return lax.dot_general(a, b, (((1,), (1,)), ((), ())), preferred_element_type=f32)


def product(a, b_hi, b_lo, mul=dot):
    hi, lo = split(a)
    rows = a.shape[0]
    both = mul(jnp.concatenate([hi, lo], axis=0), b_hi)
    return both[:rows] + (both[rows:] + mul(hi, b_lo))


def rows_of(ref, start, count):
    return ref.at[pl.ds(pl.multiple_of(start, count), count), :]


def ring_gather(buf, c, x, k, ssem, rsem):
    me = 2 * x + k
    right = 2 * lax.rem(x + 1, NX) + k
    left = 2 * lax.rem(x + NX - 1, NX) + k
    across = 2 * lax.rem(x + 2, NX) + k
    other = 2 * x + (1 - k)

    def send(block, half, slot, target):
        if half is None:
            ref = rows_of(buf, block * WIDTH, WIDTH)
        else:
            ref = rows_of(buf, block * WIDTH + half * (WIDTH // 2), WIDTH // 2)
        copy = pltpu.make_async_remote_copy(
            src_ref=ref, dst_ref=ref, send_sem=ssem.at[slot], recv_sem=rsem.at[slot],
            device_id=(c, target), device_id_type=MESH,
        )
        copy.start()
        return copy

    r0 = send(me, 0, 0, right)
    l1 = send(me, 1, 1, left)
    r1 = send(me, 1, 2, right)
    l0 = send(me, 0, 3, left)
    own = send(me, None, 4, other)
    r0.wait_recv()
    on = send(left, 0, 5, right)
    l1.wait_recv()
    back = send(right, 1, 6, left)
    r1.wait_recv()
    p_left = send(left, None, 7, other)
    l0.wait_recv()
    p_right = send(right, None, 8, other)
    on.wait_recv()
    back.wait_recv()
    p_across = send(across, None, 9, other)
    for copy in (own, p_left, p_right, p_across):
        copy.wait_recv()
    for copy in (r0, l1, r1, l0, own, on, back, p_left, p_right, p_across):
        copy.wait_send()


def kernel(
    initial, matrices, cmap_ref, low_ref, high_ref, out_ref,
    init_v, mat_v, q_ref, ah, al, cur, prev, sbuf, rbuf,
    xbuf, nh, nl, cpart, rsbuf, zbuf, corr, th, tl, root, rh, rl,
    load_sem, hs, hr, xs, xr, rs_s, rs_r, z_s, z_r, g_s, g_r, cs, cr,
):
    c = lax.axis_index("cells")
    o = lax.axis_index("orb")
    cells = NY * NZ
    x, k = o // 2, lax.rem(o, 2)
    y, z = c // NZ, lax.rem(c, NZ)
    far, near = z // NEAR, lax.rem(z, NEAR)
    g = y * NEAR + near
    after = lax.rem(c + 1, cells)
    before = lax.rem(c + cells - 1, cells)

    def member(p):
        return (p // NEAR) * NZ + far * NEAR + lax.rem(p, NEAR)

    def distant(q):
        return y * NZ + q * NEAR + near

    load_a = pltpu.make_async_copy(matrices.at[0], mat_v, load_sem.at[0])
    load_x = pltpu.make_async_copy(initial, init_v, load_sem.at[1])
    load_a.start()
    load_x.start()

    barrier = pltpu.get_barrier_semaphore()
    peers = [(distant(lax.rem(far + d, FAR)), o) for d in (4, 3, 5, 2, 6, 1, 7)]
    peers += [(member(lax.rem(g + d, GROUP)), o) for d in range(1, GROUP)]
    peers += [(after, o), (before, o)]
    peers += [
        (c, 2 * lax.rem(x + 1, NX) + k),
        (c, 2 * lax.rem(x + NX - 1, NX) + k),
        (c, 2 * x + (1 - k)),
    ]
    for peer in peers:
        pl.semaphore_signal(barrier, inc=1, device_id=peer, device_id_type=MESH)

    square = (NODE, NODE)
    down = lax.broadcasted_iota(jnp.int32, square, 0).astype(f32)
    along = lax.broadcasted_iota(jnp.int32, square, 1).astype(f32)
    eye64 = lax.broadcasted_iota(jnp.int32, (FACE, FACE), 0) == lax.broadcasted_iota(
        jnp.int32, (FACE, FACE), 1
    )

    def one_hot(mask):
        return jnp.where(mask, 1.0, 0.0).astype(bf16)

    def upright(ref):
        wide = jnp.broadcast_to(ref[...].astype(f32), (FACE, FACE))
        return jnp.sum(jnp.where(eye64, wide, 0.0), axis=1, keepdims=True)

    lanes = lax.broadcasted_iota(jnp.int32, (FACE, NODE), 1).astype(f32)
    ranks = lax.broadcasted_iota(jnp.int32, (FACE, NODE), 0).astype(f32)
    is_low = jnp.where(upright(low_ref) == lanes, 1.0, 0.0)
    is_high = jnp.where(upright(high_ref) == lanes, 1.0, 0.0)
    is_face = jnp.sum(is_low + is_high, axis=0, keepdims=True)
    face_place = jnp.sum(is_low * ranks + is_high * (ranks + FACE), axis=0, keepdims=True)
    others = jnp.broadcast_to(1.0 - is_face, (16, NODE)).astype(bf16)
    rank = dot(others, one_hot(down < along))[0:1]
    place = jnp.where(is_face > 0.5, face_place, rank + RIM)
    cmap = cmap_ref[...].astype(f32)
    at_cell = one_hot(down == cmap)
    upper = jnp.where(place >= 256.0, 1.0, 0.0)
    parts = lax.broadcasted_iota(jnp.int32, (16, NODE), 0)
    coded = jnp.where(
        parts == 0,
        jnp.broadcast_to(upper, (16, NODE)),
        jnp.broadcast_to(place - 256.0 * upper, (16, NODE)),
    ).astype(bf16)
    moved = dot(coded, at_cell)
    cell_place = moved[0:1] * 256.0 + moved[1:2]
    q_ref[...] = one_hot(down == place)
    by_cell = one_hot(down == cell_place)
    load_a.wait()
    a_hi, a_lo = split(mat_v[...])
    ah[...] = dot_t(dot(by_cell, a_hi).astype(bf16), by_cell).astype(bf16)
    al[...] = dot_t(dot(by_cell, a_lo).astype(bf16), by_cell).astype(bf16)
    load_x.wait()
    x_hi, x_lo = split(init_v[...])
    x_rest = (init_v[...] - x_hi.astype(f32) - x_lo.astype(f32)).astype(bf16)
    stacked = dot_t(jnp.concatenate([x_hi, x_lo, x_rest], axis=0), q_ref[...])
    cur[...] = stacked[0:64] + (stacked[64:128] + stacked[128:192])
    prev[...] = jnp.zeros_like(prev)

    half = WIDTH // 2
    left_lanes = lax.broadcasted_iota(jnp.int32, (half, RIM), 1) < FACE

    def to_before(rim):
        return jnp.where(left_lanes, rim[:half], pltpu.roll(rim[half:], FACE, 1))

    def to_after(rim):
        return jnp.where(left_lanes, pltpu.roll(rim[:half], FACE, 1), rim[half:])

    def halo_copy(slot, way):
        return pltpu.make_async_remote_copy(
            src_ref=sbuf.at[slot, way], dst_ref=rbuf.at[slot, way],
            send_sem=hs.at[slot, way], recv_sem=hr.at[slot, way],
            device_id=(after if way == 1 else before, o), device_id_type=MESH,
        )

    sbuf[0, 1] = to_after(cur[:, :RIM])
    pl.semaphore_wait(barrier, len(peers))
    start = halo_copy(0, 1)
    start.start()
    start.wait()
    got = rbuf[0, 1]
    first_rim = cur[:, :RIM]
    cur[:half, :RIM] = jnp.where(left_lanes, got, first_rim[:half])
    cur[half:, :RIM] = jnp.where(left_lanes, pltpu.roll(got, FACE, 1), first_rim[half:])

    def step(index, carry):
        slot = index + 1
        now = cur[...]
        hi, lo = split(now)
        both = jnp.concatenate([hi, lo], axis=0)

        def apply(begin, end):
            main = dot(both, ah[:, begin:end])
            return main[:WIDTH] + (main[WIDTH:] + dot(hi, al[:, begin:end]))

        rim = apply(0, RIM)
        sbuf[slot, 0] = to_before(rim)
        sbuf[slot, 1] = to_after(rim)
        down_copy = halo_copy(slot, 0)
        up_copy = halo_copy(slot, 1)
        down_copy.start()
        up_copy.start()
        factor = jnp.where(index == 0, 1.0, 2.0)
        inner = apply(RIM, NODE)
        following = (
            factor * (inner - center_value * now[:, RIM:]) / half_width - prev[:, RIM:]
        )
        prev[:, RIM:] = now[:, RIM:]
        cur[:, RIM:] = following
        down_copy.wait()
        up_copy.wait()
        from_next = rbuf[slot, 0]
        from_last = rbuf[slot, 1]
        add_top = jnp.where(left_lanes, from_last, pltpu.roll(from_next, FACE, 1))
        add_bottom = jnp.where(left_lanes, pltpu.roll(from_last, FACE, 1), from_next)
        image = rim + jnp.concatenate([add_top, add_bottom], axis=0)
        edge = factor * (image - center_value * now[:, :RIM]) / half_width - prev[:, :RIM]
        prev[:, :RIM] = now[:, :RIM]
        cur[:, :RIM] = edge
        return carry

    lax.fori_loop(0, DEGREE, step, 0)

    xbuf[pl.ds(pl.multiple_of(o * WIDTH, WIDTH), WIDTH), :] = cur[...]
    ring_gather(xbuf, c, x, k, xs, xr)

    e_hi, e_lo = split(xbuf[...])
    owned = lax.broadcasted_iota(jnp.int32, (WIDTH, NODE), 1) >= FACE
    cpart[...] = product(jnp.where(owned, cur[...], 0.0), e_hi, e_lo, dot_t)

    def piece(p):
        return p // 8, lax.rem(p, 8)

    def slab(ref, base, p):
        side, row = piece(p)
        return ref.at[
            pl.ds(pl.multiple_of(base + row * 8, 8), 8),
            pl.ds(pl.multiple_of(side * 256, 256), 256),
        ]

    shares = []
    for d in range(1, GROUP):
        p = lax.rem(g + d, GROUP)
        copy = pltpu.make_async_remote_copy(
            src_ref=slab(cpart, 0, p), dst_ref=rsbuf.at[g],
            send_sem=rs_s.at[d], recv_sem=rs_r.at[d],
            device_id=(member(p), o), device_id_type=MESH,
        )
        copy.start()
        shares.append(copy)
    nh[...] = dot(e_hi, q_ref[...]).astype(bf16)
    nl[...] = dot(e_lo, q_ref[...]).astype(bf16)
    side, row = piece(g)
    rsbuf[g] = cpart[
        pl.ds(pl.multiple_of(row * 8, 8), 8), pl.ds(pl.multiple_of(side * 256, 256), 256)
    ]
    for copy in shares:
        copy.wait_recv()
    zbuf[far] = jnp.sum(rsbuf[...], axis=0)
    sums = []
    for d in (4, 3, 5, 2, 6, 1, 7):
        copy = pltpu.make_async_remote_copy(
            src_ref=zbuf.at[far], dst_ref=zbuf.at[far],
            send_sem=z_s.at[d], recv_sem=z_r.at[d],
            device_id=(distant(lax.rem(far + d, FAR)), o), device_id_type=MESH,
        )
        copy.start()
        sums.append(copy)
    for copy in shares:
        copy.wait_send()
    for copy in sums:
        copy.wait_recv()
    total = jnp.sum(zbuf[...], axis=0) / float(cells * (NODE - FACE))
    mine = o * WIDTH
    corr[
        pl.ds(pl.multiple_of(mine + row * 8, 8), 8), pl.ds(pl.multiple_of(side * 256, 256), 256)
    ] = total
    spread = []
    for d in range(1, GROUP):
        ref = slab(corr, mine, g)
        copy = pltpu.make_async_remote_copy(
            src_ref=ref, dst_ref=ref, send_sem=g_s.at[d], recv_sem=g_r.at[d],
            device_id=(member(lax.rem(g + d, GROUP)), o), device_id_type=MESH,
        )
        copy.start()
        spread.append(copy)
    for copy in sums:
        copy.wait_send()
    for copy in spread:
        copy.wait_recv()
    for copy in spread:
        copy.wait_send()
    ring_gather(corr, c, x, k, cs, cr)

    full = corr[...]
    diagonal = jnp.where(down == along, full, 0.0)
    d_along = 1.0 / jnp.sqrt(jnp.sum(diagonal, axis=0, keepdims=True))
    d_down = 1.0 / jnp.sqrt(jnp.sum(diagonal, axis=1, keepdims=True))
    scaled = full * d_down * d_along
    bound = jnp.max(jnp.sum(jnp.abs(scaled), axis=1, keepdims=True), axis=0, keepdims=True)
    target = scaled / bound
    hi, lo = split(target)
    th[...] = hi
    tl[...] = lo
    root[...] = 0.5 * (jnp.where(down == along, 3.0, 0.0) - target)
    for iteration in range(NS_ITERS - 2):
        hi, lo = split(root[...])
        rh[...] = hi
        rl[...] = lo
        inner = product(root[...], rh[...], rl[...])
        in_hi, in_lo = split(inner)
        inner = product(target, in_hi, in_lo)
        in_hi, in_lo = split(inner)
        inner = product(root[...], in_hi, in_lo)
        root[...] = 0.5 * (3.0 * root[...] - inner)
    hi, lo = split(root[...])
    rh[...] = hi
    rl[...] = lo
    block = root[pl.ds(pl.multiple_of(mine, WIDTH), WIDTH), :]
    inner = product(block, rh[...], rl[...])
    inner = product(inner, th[...], tl[...])
    inner = product(inner, rh[...], rl[...])
    block = 0.5 * (3.0 * block - inner)
    mixing = block * d_along / jnp.sqrt(bound)
    out_ref[...] = product(mixing, nh[...], nl[...])


def body(initial, cell_matrices, cell_map, face_low, face_high):
    vmem = pl.BlockSpec(memory_space=pltpu.VMEM)
    hbm = pl.BlockSpec(memory_space=pl.ANY)
    dma = pltpu.SemaphoreType.DMA
    half = WIDTH // 2
    return pl.pallas_call(
        kernel,
        out_shape=jax.ShapeDtypeStruct((WIDTH, NODE), f32),
        in_specs=[hbm, hbm, vmem, vmem, vmem],
        out_specs=vmem,
        scratch_shapes=[
            pltpu.VMEM((WIDTH, NODE), f32),
            pltpu.VMEM((NODE, NODE), f32),
            pltpu.VMEM((NODE, NODE), bf16),
            pltpu.VMEM((NODE, NODE), bf16),
            pltpu.VMEM((NODE, NODE), bf16),
            pltpu.VMEM((WIDTH, NODE), f32),
            pltpu.VMEM((WIDTH, NODE), f32),
            pltpu.VMEM((DEGREE + 1, 2, half, RIM), f32),
            pltpu.VMEM((DEGREE + 1, 2, half, RIM), f32),
            pltpu.VMEM((NORB, NODE), f32),
            pltpu.VMEM((NORB, NODE), bf16),
            pltpu.VMEM((NORB, NODE), bf16),
            pltpu.VMEM((WIDTH, NORB), f32),
            pltpu.VMEM((GROUP, 8, 256), f32),
            pltpu.VMEM((FAR, 8, 256), f32),
            pltpu.VMEM((NORB, NORB), f32),
            pltpu.VMEM((NORB, NORB), bf16),
            pltpu.VMEM((NORB, NORB), bf16),
            pltpu.VMEM((NORB, NORB), f32),
            pltpu.VMEM((NORB, NORB), bf16),
            pltpu.VMEM((NORB, NORB), bf16),
            dma((2,)),
            dma((DEGREE + 1, 2)), dma((DEGREE + 1, 2)),
            dma((10,)), dma((10,)),
            dma((GROUP,)), dma((GROUP,)),
            dma((FAR,)), dma((FAR,)),
            dma((GROUP,)), dma((GROUP,)),
            dma((10,)), dma((10,)),
        ],
        compiler_params=pltpu.CompilerParams(collective_id=0, has_side_effects=True),
        name="subspace_step",
    )(initial, cell_matrices, cell_map, face_low, face_high)


def solution(mesh):
    placed = (
        P("orb", "cells"),
        P("cells", None, None),
        P("cells", None),
        P("cells", None),
        P("cells", None),
    )
    return jax.shard_map(
        body, mesh=mesh, in_specs=placed, out_specs=P("orb", "cells"), check_vma=False
    )
```

time: 809 us -> 112 us (0.14)
  waiting for transfers between devices: 613 us -> 0 us
  Pallas kernels: 0 us -> 110 us
  starting transfers between devices: 85.6 us -> 0 us
  other arithmetic: 37.6 us -> 0 us
  local copies, waits for them, and re-layouts: 29.2 us -> 1.57 us
  matrix products: 20.9 us -> 0 us
  between operations: 15 us -> 0.01 us
    psum x1 -> x0, waiting for transfers between devices: 485 us -> none  [body(): column_block = lax.psum(local_terms, 'cells') / owned_count]
    all_gather x3 -> x0, waiting for transfers between devices: 128 us -> none  [the longest x1 53.1 us: body(): correlation = lax.all_gather(column_block, 'orb', axis=1, tiled=True)]
    pallas_call x0 -> x1, Pallas kernels: none -> 110 us  [body(): pl.pallas_call(kernel, out_shape=jax.ShapeDtypeStruct((WIDTH, NODE), f32)...]
    ppermute x16 -> x0, starting transfers between devices: 85.2 us -> none  [the longest x8 67.5 us: with_halo(): lax.ppermute(lax.slice_in_dim(block, 0, width, axis=dim), axis, backward)]
    scatter-add x23 -> x0, other arithmetic: 33.1 us -> none  [the longest x7 16.2 us: apply_operator(): summed = jnp.zeros_like(values).at[:, cell_map].add(product)]
    gather x24 -> x0, local copies, waits for them, and re-layouts: 25.3 us -> none  [the longest x16 9.54 us: assemble(): rims = jnp.stack([values[:, lower_index], values[:, upper_index]])]
    dot_general x15 -> x0, matrix products: 20.9 us -> none  [the longest x7 8.16 us: apply_operator(): product = jnp.einsum('ocn,cmn->ocm', gathered, matrices, precision=highest)]
  transfers between devices with their start and end apart: 20 -> 0, of which waited for: 4 -> 0; matrix products, arithmetic and copies ran while one was open for 1% -> 0% of each run, Pallas kernels for 0% -> 0%
where the time goes in v1:
time: 112 us
  Pallas kernels  110 us (98%)
  local copies, waits for them, and re-layouts  1.57 us (1%)
    pallas_call x1, Pallas kernels, body(): pl.pallas_call(kernel, out_shape=jax.ShapeDtypeStruct((WIDTH, NODE), f32)...  110 us

profile of v1, /device:TPU:1, one launch (start us, length us, event | category | flops | bytes accessed | tf_op | source)
XLA Modules:
  0.0 111.6 jit_solution(95242154926377223)
XLA Ops:
  0.0 110.0 %subspace_step.1 = f32[64,512]{1,0:T(8,128)} custom-call(f32[64,512]{1,0:T(8,128)} %initial.1, f32[1,512,512]{2,1,0:T(8,128)} %matrices.1, s32[1,512]{1,0:T(1,128)} %cmap_ref.1, s32[1,64]{1,0:T(1,128)} %low_ref.1, s32[1,64]{1,0:T(1,128)} %high_ref.1), custom_call_target="tpu_custom_call" | custom-call | tf_op jit(solution)/shard_map/subspace_step/pallas_call | solution.py:349
  110.0 1.6 %copy.7 = f32[64,512]{1,0:T(8,128)} copy(f32[64,512]{1,0:T(8,128)} %subspace_step.1) | data formatting | bytes 262144

commit v2 on v1

--- a/solution.py
+++ b/solution.py
@@ -89,9 +89,9 @@
 
 def kernel(
     initial, matrices, cmap_ref, low_ref, high_ref, out_ref,
-    init_v, mat_v, q_ref, ah, al, cur, prev, sbuf, rbuf,
+    init_v, mat_v, q_ref, ah, al, cur, prev, image, sbuf, rbuf,
     xbuf, nh, nl, cpart, rsbuf, zbuf, corr, th, tl, root, rh, rl,
-    load_sem, hs, hr, xs, xr, rs_s, rs_r, z_s, z_r, g_s, g_r, cs, cr,
+    load_sem, hs, hr, xs, xr, rs_s, rs_r, z_s, z_r, g_s, g_r, cs, cr, far_sem,
 ):
     c = lax.axis_index("cells")
     o = lax.axis_index("orb")
@@ -115,8 +115,13 @@
     load_x.start()
 
     barrier = pltpu.get_barrier_semaphore()
-    peers = [(distant(lax.rem(far + d, FAR)), o) for d in (4, 3, 5, 2, 6, 1, 7)]
-    peers += [(member(lax.rem(g + d, GROUP)), o) for d in range(1, GROUP)]
+    def ring_z(d):
+        return (y * NZ + lax.rem(z + d + NZ, NZ), o)
+
+    def ring_y(d):
+        return (lax.rem(y + d + NY, NY) * NZ + z, o)
+
+    peers = [ring_z(1), ring_z(-1), ring_y(1), ring_y(-1)]
     peers += [(after, o), (before, o)]
     peers += [
         (c, 2 * lax.rem(x + 1, NX) + k),
@@ -149,6 +154,45 @@
     others = jnp.broadcast_to(1.0 - is_face, (16, NODE)).astype(bf16)
     rank = dot(others, one_hot(down < along))[0:1]
     place = jnp.where(is_face > 0.5, face_place, rank + RIM)
+    q_ref[...] = one_hot(down == place)
+    load_x.wait()
+    x_hi, x_lo = split(init_v[...])
+    x_rest = (init_v[...] - x_hi.astype(f32) - x_lo.astype(f32)).astype(bf16)
+    stacked = dot_t(jnp.concatenate([x_hi, x_lo, x_rest], axis=0), q_ref[...])
+    cur[...] = stacked[0:64] + (stacked[64:128] + stacked[128:192])
+    prev[...] = jnp.zeros_like(prev)
+
+    half = WIDTH // 2
+    left_lanes = lax.broadcasted_iota(jnp.int32, (half, RIM), 1) < FACE
+
+    def to_before(rim):
+        return jnp.where(left_lanes, rim[:half], pltpu.roll(rim[half:], FACE, 1))
+
+    def to_after(rim):
+        return jnp.where(left_lanes, pltpu.roll(rim[:half], FACE, 1), rim[half:])
+
+    def halo_copy(slot, way):
+        return pltpu.make_async_remote_copy(
+            src_ref=sbuf.at[slot, way], dst_ref=rbuf.at[slot, way],
+            send_sem=hs.at[slot, way], recv_sem=hr.at[slot, way],
+            device_id=(after if way == 1 else before, o), device_id_type=MESH,
+        )
+
+    sbuf[0, 1] = to_after(cur[:, :RIM])
+    pl.semaphore_wait(barrier, len(peers))
+    start = halo_copy(0, 1)
+    start.start()
+    stages = [ring_z(1), ring_z(-1)], [ring_z(2), ring_z(-2)], [ring_z(4), ring_z(-4)]
+    stages += ([ring_z(8), ring_z(-8)], [ring_y(1), ring_y(-1)], [ring_y(1), ring_y(-1)])
+
+    def greet(stage):
+        for peer in stages[stage]:
+            pl.semaphore_signal(far_sem.at[stage], inc=1, device_id=peer, device_id_type=MESH)
+
+    def greeted(stage):
+        pl.semaphore_wait(far_sem.at[stage], 2)
+
+    greet(0)
     cmap = cmap_ref[...].astype(f32)
     at_cell = one_hot(down == cmap)
     upper = jnp.where(place >= 256.0, 1.0, 0.0)
@@ -160,39 +204,22 @@
     ).astype(bf16)
     moved = dot(coded, at_cell)
     cell_place = moved[0:1] * 256.0 + moved[1:2]
-    q_ref[...] = one_hot(down == place)
     by_cell = one_hot(down == cell_place)
     load_a.wait()
     a_hi, a_lo = split(mat_v[...])
     ah[...] = dot_t(dot(by_cell, a_hi).astype(bf16), by_cell).astype(bf16)
     al[...] = dot_t(dot(by_cell, a_lo).astype(bf16), by_cell).astype(bf16)
-    load_x.wait()
-    x_hi, x_lo = split(init_v[...])
-    x_rest = (init_v[...] - x_hi.astype(f32) - x_lo.astype(f32)).astype(bf16)
-    stacked = dot_t(jnp.concatenate([x_hi, x_lo, x_rest], axis=0), q_ref[...])
-    cur[...] = stacked[0:64] + (stacked[64:128] + stacked[128:192])
-    prev[...] = jnp.zeros_like(prev)
-
-    half = WIDTH // 2
-    left_lanes = lax.broadcasted_iota(jnp.int32, (half, RIM), 1) < FACE
-
-    def to_before(rim):
-        return jnp.where(left_lanes, rim[:half], pltpu.roll(rim[half:], FACE, 1))
-
-    def to_after(rim):
-        return jnp.where(left_lanes, pltpu.roll(rim[:half], FACE, 1), rim[half:])
-
-    def halo_copy(slot, way):
-        return pltpu.make_async_remote_copy(
-            src_ref=sbuf.at[slot, way], dst_ref=rbuf.at[slot, way],
-            send_sem=hs.at[slot, way], recv_sem=hr.at[slot, way],
-            device_id=(after if way == 1 else before, o), device_id_type=MESH,
-        )
-
-    sbuf[0, 1] = to_after(cur[:, :RIM])
-    pl.semaphore_wait(barrier, len(peers))
-    start = halo_copy(0, 1)
-    start.start()
+
+    def apply(a, begin, end, first, last):
+        hi, lo = split(a)
+        rows = slice(begin, end)
+        main = dot(jnp.concatenate([hi, lo], axis=0), ah[rows, first:last])
+        return main[:WIDTH] + (main[WIDTH:] + dot(hi, al[rows, first:last]))
+
+    def ahead():
+        image[...] = apply(cur[:, RIM:], RIM, NODE, 0, NODE)
+
+    ahead()
     start.wait()
     got = rbuf[0, 1]
     first_rim = cur[:, :RIM]
@@ -201,37 +228,35 @@
 
     def step(index, carry):
         slot = index + 1
-        now = cur[...]
-        hi, lo = split(now)
-        both = jnp.concatenate([hi, lo], axis=0)
-
-        def apply(begin, end):
-            main = dot(both, ah[:, begin:end])
-            return main[:WIDTH] + (main[WIDTH:] + dot(hi, al[:, begin:end]))
-
-        rim = apply(0, RIM)
+        now = cur[:, :RIM]
+        rim = image[:, :RIM] + apply(now, 0, RIM, 0, RIM)
         sbuf[slot, 0] = to_before(rim)
         sbuf[slot, 1] = to_after(rim)
         down_copy = halo_copy(slot, 0)
         up_copy = halo_copy(slot, 1)
         down_copy.start()
         up_copy.start()
+        for stage, when in enumerate((0, 1, 2, 4, 5)):
+            @pl.when(index == when)
+            def _():
+                greeted(stage)
+                greet(stage + 1)
         factor = jnp.where(index == 0, 1.0, 2.0)
-        inner = apply(RIM, NODE)
-        following = (
-            factor * (inner - center_value * now[:, RIM:]) / half_width - prev[:, RIM:]
-        )
-        prev[:, RIM:] = now[:, RIM:]
+        inner = image[:, RIM:] + apply(now, 0, RIM, RIM, NODE)
+        core = cur[:, RIM:]
+        following = factor * (inner - center_value * core) / half_width - prev[:, RIM:]
+        prev[:, RIM:] = core
         cur[:, RIM:] = following
+        ahead()
         down_copy.wait()
         up_copy.wait()
         from_next = rbuf[slot, 0]
         from_last = rbuf[slot, 1]
         add_top = jnp.where(left_lanes, from_last, pltpu.roll(from_next, FACE, 1))
         add_bottom = jnp.where(left_lanes, pltpu.roll(from_last, FACE, 1), from_next)
-        image = rim + jnp.concatenate([add_top, add_bottom], axis=0)
-        edge = factor * (image - center_value * now[:, :RIM]) / half_width - prev[:, :RIM]
-        prev[:, :RIM] = now[:, :RIM]
+        rim = rim + jnp.concatenate([add_top, add_bottom], axis=0)
+        edge = factor * (rim - center_value * now) / half_width - prev[:, :RIM]
+        prev[:, :RIM] = now
         cur[:, :RIM] = edge
         return carry
 
@@ -239,6 +264,7 @@
 
     xbuf[pl.ds(pl.multiple_of(o * WIDTH, WIDTH), WIDTH), :] = cur[...]
     ring_gather(xbuf, c, x, k, xs, xr)
+    greeted(5)
 
     e_hi, e_lo = split(xbuf[...])
     owned = lax.broadcasted_iota(jnp.int32, (WIDTH, NODE), 1) >= FACE
@@ -359,6 +385,7 @@
             pltpu.VMEM((NODE, NODE), bf16),
             pltpu.VMEM((WIDTH, NODE), f32),
             pltpu.VMEM((WIDTH, NODE), f32),
+            pltpu.VMEM((WIDTH, NODE), f32),
             pltpu.VMEM((DEGREE + 1, 2, half, RIM), f32),
             pltpu.VMEM((DEGREE + 1, 2, half, RIM), f32),
             pltpu.VMEM((NORB, NODE), f32),
@@ -380,6 +407,7 @@
             dma((FAR,)), dma((FAR,)),
             dma((GROUP,)), dma((GROUP,)),
             dma((10,)), dma((10,)),
+            pltpu.SemaphoreType.REGULAR((6,)),
         ],
         compiler_params=pltpu.CompilerParams(collective_id=0, has_side_effects=True),
         name="subspace_step",

time: 112 us -> 102 us (0.911)
  Pallas kernels: 110 us -> 100 us
    pallas_call x1, Pallas kernels: 110 us -> 100 us  [body(): pl.pallas_call(kernel, out_shape=jax.ShapeDtypeStruct((WIDTH, NODE), f32)...]
where the time goes in v2:
time: 102 us
  Pallas kernels  100 us (98%)
  local copies, waits for them, and re-layouts  1.57 us (2%)
    pallas_call x1, Pallas kernels, body(): pl.pallas_call(kernel, out_shape=jax.ShapeDtypeStruct((WIDTH, NODE), f32)...  100 us

profile of v2, /device:TPU:1, one launch (start us, length us, event | category | flops | bytes accessed | tf_op | source)
XLA Modules:
  0.0 101.7 jit_solution(9794125931605060024)
XLA Ops:
  0.0 100.1 %subspace_step.1 = f32[64,512]{1,0:T(8,128)} custom-call(f32[64,512]{1,0:T(8,128)} %initial.1, f32[1,512,512]{2,1,0:T(8,128)} %matrices.1, s32[1,512]{1,0:T(1,128)} %cmap_ref.1, s32[1,64]{1,0:T(1,128)} %low_ref.1, s32[1,64]{1,0:T(1,128)} %high_ref.1), custom_call_target="tpu_custom_call" | custom-call | tf_op jit(solution)/shard_map/subspace_step/pallas_call | solution.py:375
  100.1 1.6 %copy.7 = f32[64,512]{1,0:T(8,128)} copy(f32[64,512]{1,0:T(8,128)} %subspace_step.1) | data formatting | bytes 262144

commit v3 on v2

--- a/solution.py
+++ b/solution.py
@@ -42,22 +42,13 @@
     return both[:rows] + (both[rows:] + mul(hi, b_lo))
 
 
-def rows_of(ref, start, count):
-    return ref.at[pl.ds(pl.multiple_of(start, count), count), :]
-
-
-def ring_gather(buf, c, x, k, ssem, rsem):
-    me = 2 * x + k
-    right = 2 * lax.rem(x + 1, NX) + k
-    left = 2 * lax.rem(x + NX - 1, NX) + k
-    across = 2 * lax.rem(x + 2, NX) + k
-    other = 2 * x + (1 - k)
+def ring_gather(view, c, x, k, ssem, rsem, first, second, passing):
+    right_x, left_x = lax.rem(x + 1, NX), lax.rem(x + NX - 1, NX)
+    across = lax.rem(x + 2, NX)
+    right, left, other = 2 * right_x + k, 2 * left_x + k, 2 * x + (1 - k)
 
     def send(block, half, slot, target):
-        if half is None:
-            ref = rows_of(buf, block * WIDTH, WIDTH)
-        else:
-            ref = rows_of(buf, block * WIDTH + half * (WIDTH // 2), WIDTH // 2)
+        ref = view(block, half)
         copy = pltpu.make_async_remote_copy(
             src_ref=ref, dst_ref=ref, send_sem=ssem.at[slot], recv_sem=rsem.at[slot],
             device_id=(c, target), device_id_type=MESH,
@@ -65,26 +56,33 @@
         copy.start()
         return copy
 
-    r0 = send(me, 0, 0, right)
-    l1 = send(me, 1, 1, left)
-    r1 = send(me, 1, 2, right)
-    l0 = send(me, 0, 3, left)
-    own = send(me, None, 4, other)
+    passed = []
+
+    def pass_over(block, half):
+        if half in passing:
+            passed.append(send(block, (first, second)[half], 6 + len(passed), other))
+
+    r0 = send(x, first, 0, right)
+    l1 = send(x, second, 1, left)
+    pass_over(x, 0)
+    pass_over(x, 1)
+    r1 = send(x, second, 2, right)
+    l0 = send(x, first, 3, left)
     r0.wait_recv()
-    on = send(left, 0, 5, right)
+    on = send(left_x, first, 4, right)
+    pass_over(left_x, 0)
     l1.wait_recv()
-    back = send(right, 1, 6, left)
+    back = send(right_x, second, 5, left)
+    pass_over(right_x, 1)
     r1.wait_recv()
-    p_left = send(left, None, 7, other)
+    pass_over(left_x, 1)
     l0.wait_recv()
-    p_right = send(right, None, 8, other)
+    pass_over(right_x, 0)
     on.wait_recv()
+    pass_over(across, 0)
     back.wait_recv()
-    p_across = send(across, None, 9, other)
-    for copy in (own, p_left, p_right, p_across):
-        copy.wait_recv()
-    for copy in (r0, l1, r1, l0, own, on, back, p_left, p_right, p_across):
-        copy.wait_send()
+    pass_over(across, 1)
+    return [r0, l1, r1, l0, on, back], passed
 
 
 def kernel(
@@ -262,40 +260,42 @@
 
     lax.fori_loop(0, DEGREE, step, 0)
 
-    xbuf[pl.ds(pl.multiple_of(o * WIDTH, WIDTH), WIDTH), :] = cur[...]
-    ring_gather(xbuf, c, x, k, xs, xr)
+    mine = (k * NX + x) * WIDTH
+
+    def orbitals(block, part):
+        start = (k * NX + block) * WIDTH + part * half
+        return xbuf.at[pl.ds(pl.multiple_of(start, half), half), :]
+
+    xbuf[pl.ds(pl.multiple_of(mine, WIDTH), WIDTH), :] = cur[...]
+    x_sent, x_passed = ring_gather(orbitals, c, x, k, xs, xr, 0, 1, (0, 1))
     greeted(5)
-
-    e_hi, e_lo = split(xbuf[...])
-    owned = lax.broadcasted_iota(jnp.int32, (WIDTH, NODE), 1) >= FACE
-    cpart[...] = product(jnp.where(owned, cur[...], 0.0), e_hi, e_lo, dot_t)
-
-    def piece(p):
-        return p // 8, lax.rem(p, 8)
-
-    def slab(ref, base, p):
-        side, row = piece(p)
-        return ref.at[
-            pl.ds(pl.multiple_of(base + row * 8, 8), 8),
-            pl.ds(pl.multiple_of(side * 256, 256), 256),
-        ]
-
+    for copy in x_passed[:2]:
+        copy.wait_recv()
+
+    side = pl.ds(pl.multiple_of(k * 256, 256), 256)
+    e_hi, e_lo = split(xbuf[side, :])
+    owned = lax.broadcasted_iota(jnp.int32, (2 * WIDTH, NODE), 1) >= FACE
+    chip = jnp.concatenate(
+        [xbuf[pl.ds(pl.multiple_of(b * 256 + x * WIDTH, WIDTH), WIDTH), :] for b in (0, 1)], axis=0
+    )
+    cpart[...] = product(jnp.where(owned, chip, 0.0), e_hi, e_lo, dot_t)
+
+    def slab(p):
+        row = (p // 8) * 256 + x * WIDTH + lax.rem(p, 8) * 8
+        return pl.ds(pl.multiple_of(row, 8), 8)
+
+    own_slab = pl.ds(pl.multiple_of(g * 8, 8), 8)
     shares = []
     for d in range(1, GROUP):
         p = lax.rem(g + d, GROUP)
         copy = pltpu.make_async_remote_copy(
-            src_ref=slab(cpart, 0, p), dst_ref=rsbuf.at[g],
+            src_ref=cpart.at[pl.ds(pl.multiple_of(p * 8, 8), 8), :], dst_ref=rsbuf.at[g],
             send_sem=rs_s.at[d], recv_sem=rs_r.at[d],
             device_id=(member(p), o), device_id_type=MESH,
         )
         copy.start()
         shares.append(copy)
-    nh[...] = dot(e_hi, q_ref[...]).astype(bf16)
-    nl[...] = dot(e_lo, q_ref[...]).astype(bf16)
-    side, row = piece(g)
-    rsbuf[g] = cpart[
-        pl.ds(pl.multiple_of(row * 8, 8), 8), pl.ds(pl.multiple_of(side * 256, 256), 256)
-    ]
+    rsbuf[g] = cpart[own_slab, :]
     for copy in shares:
         copy.wait_recv()
     zbuf[far] = jnp.sum(rsbuf[...], axis=0)
@@ -308,18 +308,20 @@
         )
         copy.start()
         sums.append(copy)
-    for copy in shares:
+    for copy in x_passed[2:]:
+        copy.wait_recv()
+    e_hi, e_lo = split(xbuf[...])
+    nh[...] = dot(e_hi, q_ref[...]).astype(bf16)
+    nl[...] = dot(e_lo, q_ref[...]).astype(bf16)
+    for copy in shares + x_sent + x_passed:
         copy.wait_send()
     for copy in sums:
         copy.wait_recv()
     total = jnp.sum(zbuf[...], axis=0) / float(cells * (NODE - FACE))
-    mine = o * WIDTH
-    corr[
-        pl.ds(pl.multiple_of(mine + row * 8, 8), 8), pl.ds(pl.multiple_of(side * 256, 256), 256)
-    ] = total
+    corr[k, slab(g)] = total
     spread = []
     for d in range(1, GROUP):
-        ref = slab(corr, mine, g)
+        ref = corr.at[k, slab(g)]
         copy = pltpu.make_async_remote_copy(
             src_ref=ref, dst_ref=ref, send_sem=g_s.at[d], recv_sem=g_r.at[d],
             device_id=(member(lax.rem(g + d, GROUP)), o), device_id_type=MESH,
@@ -332,9 +334,19 @@
         copy.wait_recv()
     for copy in spread:
         copy.wait_send()
-    ring_gather(corr, c, x, k, cs, cr)
-
-    full = corr[...]
+
+    def quarter(block, part):
+        return corr.at[k, pl.ds(pl.multiple_of(part * 256 + block * WIDTH, WIDTH), WIDTH)]
+
+    c_sent, c_passed = ring_gather(quarter, c, x, k, cs, cr, k, 1 - k, (0,))
+    off_side = pl.ds(pl.multiple_of((1 - k) * 256, 256), 256)
+    corr[1 - k, side] = corr[k, off_side].T
+    for copy in c_passed:
+        copy.wait_recv()
+    for copy in c_sent + c_passed:
+        copy.wait_send()
+
+    full = jnp.concatenate([corr[0], corr[1]], axis=1)
     diagonal = jnp.where(down == along, full, 0.0)
     d_along = 1.0 / jnp.sqrt(jnp.sum(diagonal, axis=0, keepdims=True))
     d_down = 1.0 / jnp.sqrt(jnp.sum(diagonal, axis=1, keepdims=True))
@@ -391,10 +403,10 @@
             pltpu.VMEM((NORB, NODE), f32),
             pltpu.VMEM((NORB, NODE), bf16),
             pltpu.VMEM((NORB, NODE), bf16),
-            pltpu.VMEM((WIDTH, NORB), f32),
+            pltpu.VMEM((2 * WIDTH, 256), f32),
             pltpu.VMEM((GROUP, 8, 256), f32),
             pltpu.VMEM((FAR, 8, 256), f32),
-            pltpu.VMEM((NORB, NORB), f32),
+            pltpu.VMEM((2, NORB, 256), f32),
             pltpu.VMEM((NORB, NORB), bf16),
             pltpu.VMEM((NORB, NORB), bf16),
             pltpu.VMEM((NORB, NORB), f32),
@@ -402,7 +414,7 @@
             pltpu.VMEM((NORB, NORB), bf16),
             dma((2,)),
             dma((DEGREE + 1, 2)), dma((DEGREE + 1, 2)),
-            dma((10,)), dma((10,)),
+            dma((14,)), dma((14,)),
             dma((GROUP,)), dma((GROUP,)),
             dma((FAR,)), dma((FAR,)),
             dma((GROUP,)), dma((GROUP,)),

time: 102 us -> 98.9 us (0.970)
  Pallas kernels: 100 us -> 97.1 us
    pallas_call x1, Pallas kernels: 100 us -> 97.1 us  [body(): pl.pallas_call(kernel, out_shape=jax.ShapeDtypeStruct((WIDTH, NODE), f32)...]
where the time goes in v3:
time: 98.9 us; the launch traced here: 98.7 us
  Pallas kernels  97.1 us (98%)
  local copies, waits for them, and re-layouts  1.57 us (2%)
    pallas_call x1, Pallas kernels, body(): pl.pallas_call(kernel, out_shape=jax.ShapeDtypeStruct((WIDTH, NODE), f32)...  97.1 us

profile of v3, /device:TPU:1, one launch (start us, length us, event | category | flops | bytes accessed | tf_op | source)
XLA Modules:
  0.0 98.7 jit_solution(11595156731050309985)
XLA Ops:
  0.0 97.1 %subspace_step.1 = f32[64,512]{1,0:T(8,128)} custom-call(f32[64,512]{1,0:T(8,128)} %initial.1, f32[1,512,512]{2,1,0:T(8,128)} %matrices.1, s32[1,512]{1,0:T(1,128)} %cmap_ref.1, s32[1,64]{1,0:T(1,128)} %low_ref.1, s32[1,64]{1,0:T(1,128)} %high_ref.1), custom_call_target="tpu_custom_call" | custom-call | tf_op jit(solution)/shard_map/subspace_step/pallas_call | solution.py:387
  97.1 1.6 %copy.7 = f32[64,512]{1,0:T(8,128)} copy(f32[64,512]{1,0:T(8,128)} %subspace_step.1) | data formatting | bytes 262144

commit v4 on v3

--- a/solution.py
+++ b/solution.py
@@ -88,8 +88,10 @@
 def kernel(
     initial, matrices, cmap_ref, low_ref, high_ref, out_ref,
     init_v, mat_v, q_ref, ah, al, cur, prev, image, sbuf, rbuf,
+    block_out, block_in, fbuf, fgot, nbuf, ngot,
     xbuf, nh, nl, cpart, rsbuf, zbuf, corr, th, tl, root, rh, rl,
-    load_sem, hs, hr, xs, xr, rs_s, rs_r, z_s, z_r, g_s, g_r, cs, cr, far_sem,
+    load_sem, hs, hr, xs, xr, rs_s, rs_r, z_s, z_r, g_s, g_r, cs, cr,
+    bs, br, fs, fr, ns, nr, far_sem,
 ):
     c = lax.axis_index("cells")
     o = lax.axis_index("orb")
@@ -182,6 +184,7 @@
     start.start()
     stages = [ring_z(1), ring_z(-1)], [ring_z(2), ring_z(-2)], [ring_z(4), ring_z(-4)]
     stages += ([ring_z(8), ring_z(-8)], [ring_y(1), ring_y(-1)], [ring_y(1), ring_y(-1)])
+    stages += ([(after, o), (before, o)],)
 
     def greet(stage):
         for peer in stages[stage]:
@@ -191,6 +194,7 @@
         pl.semaphore_wait(far_sem.at[stage], 2)
 
     greet(0)
+    greet(6)
     cmap = cmap_ref[...].astype(f32)
     at_cell = one_hot(down == cmap)
     upper = jnp.where(place >= 256.0, 1.0, 0.0)
@@ -217,6 +221,18 @@
     def ahead():
         image[...] = apply(cur[:, RIM:], RIM, NODE, 0, NODE)
 
+    block_out[...] = ah[:RIM, :RIM].astype(f32) + al[:RIM, :RIM].astype(f32)
+
+    def neighbour_copy(source, target, send, recv, slot, way, distance):
+        to = lax.rem(c + (distance if way == 1 else cells - distance), cells)
+        return pltpu.make_async_remote_copy(
+            src_ref=source, dst_ref=target, send_sem=send.at[slot, way],
+            recv_sem=recv.at[slot, way], device_id=(to, o), device_id_type=MESH,
+        )
+
+    blocks = [neighbour_copy(block_out, block_in.at[w], bs, br, 0, w, 1) for w in (0, 1)]
+    for copy in blocks:
+        copy.start()
     ahead()
     start.wait()
     got = rbuf[0, 1]
@@ -234,18 +250,14 @@
         up_copy = halo_copy(slot, 1)
         down_copy.start()
         up_copy.start()
-        for stage, when in enumerate((0, 1, 2, 4, 5)):
-            @pl.when(index == when)
-            def _():
-                greeted(stage)
-                greet(stage + 1)
-        factor = jnp.where(index == 0, 1.0, 2.0)
+        greeted(0)
+        greet(1)
+        factor = 1.0
         inner = image[:, RIM:] + apply(now, 0, RIM, RIM, NODE)
         core = cur[:, RIM:]
         following = factor * (inner - center_value * core) / half_width - prev[:, RIM:]
         prev[:, RIM:] = core
         cur[:, RIM:] = following
-        ahead()
         down_copy.wait()
         up_copy.wait()
         from_next = rbuf[slot, 0]
@@ -258,7 +270,76 @@
         cur[:, :RIM] = edge
         return carry
 
-    lax.fori_loop(0, DEGREE, step, 0)
+    step(0, 0)
+    greeted(6)
+    for copy in blocks:
+        copy.wait()
+    wide_left = lax.broadcasted_iota(jnp.int32, (WIDTH, RIM), 1) < FACE
+    scale = 2.0 / half_width
+
+    def times_block(a, way):
+        b_hi, b_lo = split(block_in[way])
+        return product(a, b_hi, b_lo)
+
+    def two_steps(index, carry):
+        now, last = cur[...], prev[...]
+        image[...] = apply(now, 0, NODE, 0, NODE)
+        rim = image[:, :RIM]
+        fbuf[index, 0] = to_before(rim)
+        fbuf[index, 1] = to_after(rim)
+        two = [
+            neighbour_copy(fbuf.at[index, w], fgot.at[index, w], fs, fr, index, w, 2) for w in (0, 1)
+        ]
+        for copy in two:
+            copy.start()
+        part = scale * (image[...] - center_value * now) - last
+        prev[...] = part
+        second = apply(part, 0, NODE, 0, RIM)
+        turned = pltpu.roll(second, FACE, 1)
+        nbuf[index, 0] = jnp.where(wide_left, rim, turned)
+        nbuf[index, 1] = jnp.where(wide_left, turned, rim)
+        one = [
+            neighbour_copy(nbuf.at[index, w], ngot.at[index, w], ns, nr, index, w, 1) for w in (0, 1)
+        ]
+        for copy in one:
+            copy.start()
+        for stage in (1, 2, 3):
+            @pl.when(index == stage - 1)
+            def _():
+                greeted(stage)
+                greet(stage + 1)
+        image[:, :RIM] = second
+        image[:, RIM:] = apply(part, 0, NODE, RIM, NODE)
+        swapped = pltpu.roll(rim, FACE, 1)
+        for copy in two:
+            copy.wait()
+        far_next = fgot[index, 0]
+        far_last = fgot[index, 1]
+        to_last = jnp.concatenate([
+            jnp.where(left_lanes, far_last, swapped[:half]),
+            jnp.where(left_lanes, pltpu.roll(far_last, FACE, 1), swapped[half:]),
+        ], axis=0)
+        to_next = jnp.concatenate([
+            jnp.where(left_lanes, swapped[:half], pltpu.roll(far_next, FACE, 1)),
+            jnp.where(left_lanes, swapped[half:], far_next),
+        ], axis=0)
+        through = jnp.where(wide_left, times_block(to_next, 0), times_block(to_last, 1))
+        through = scale * pltpu.roll(through, FACE, 1)
+        for copy in one:
+            copy.wait()
+        from_next = ngot[index, 0]
+        from_last = ngot[index, 1]
+        received = scale * pltpu.roll(jnp.where(wide_left, from_next, from_last), FACE, 1)
+        later = jnp.where(wide_left, from_last, from_next) + through
+        image[...] = image[...] + apply(received, 0, RIM, 0, NODE)
+        image[:, :RIM] = image[:, :RIM] + later
+        prev[:, :RIM] = prev[:, :RIM] + received
+        cur[...] = scale * (image[...] - center_value * prev[...]) - now
+        return carry
+
+    lax.fori_loop(0, (DEGREE - 1) // 2, two_steps, 0)
+    greeted(4)
+    greet(5)
 
     mine = (k * NX + x) * WIDTH
 
@@ -398,8 +479,14 @@
             pltpu.VMEM((WIDTH, NODE), f32),
             pltpu.VMEM((WIDTH, NODE), f32),
             pltpu.VMEM((WIDTH, NODE), f32),
-            pltpu.VMEM((DEGREE + 1, 2, half, RIM), f32),
-            pltpu.VMEM((DEGREE + 1, 2, half, RIM), f32),
+            pltpu.VMEM((2, 2, half, RIM), f32),
+            pltpu.VMEM((2, 2, half, RIM), f32),
+            pltpu.VMEM((RIM, RIM), f32),
+            pltpu.VMEM((2, RIM, RIM), f32),
+            pltpu.VMEM((DEGREE // 2, 2, half, RIM), f32),
+            pltpu.VMEM((DEGREE // 2, 2, half, RIM), f32),
+            pltpu.VMEM((DEGREE // 2, 2, WIDTH, RIM), f32),
+            pltpu.VMEM((DEGREE // 2, 2, WIDTH, RIM), f32),
             pltpu.VMEM((NORB, NODE), f32),
             pltpu.VMEM((NORB, NODE), bf16),
             pltpu.VMEM((NORB, NODE), bf16),
@@ -413,13 +500,16 @@
             pltpu.VMEM((NORB, NORB), bf16),
             pltpu.VMEM((NORB, NORB), bf16),
             dma((2,)),
-            dma((DEGREE + 1, 2)), dma((DEGREE + 1, 2)),
+            dma((2, 2)), dma((2, 2)),
             dma((14,)), dma((14,)),
             dma((GROUP,)), dma((GROUP,)),
             dma((FAR,)), dma((FAR,)),
             dma((GROUP,)), dma((GROUP,)),
             dma((10,)), dma((10,)),
-            pltpu.SemaphoreType.REGULAR((6,)),
+            dma((1, 2)), dma((1, 2)),
+            dma((DEGREE // 2, 2)), dma((DEGREE // 2, 2)),
+            dma((DEGREE // 2, 2)), dma((DEGREE // 2, 2)),
+            pltpu.SemaphoreType.REGULAR((7,)),
         ],
         compiler_params=pltpu.CompilerParams(collective_id=0, has_side_effects=True),
         name="subspace_step",

time: 98.9 us -> 91.5 us (0.925)
  Pallas kernels: 97.1 us -> 89.7 us
    pallas_call x1, Pallas kernels: 97.1 us -> 89.7 us  [body(): pl.pallas_call(kernel, out_shape=jax.ShapeDtypeStruct((WIDTH, NODE), f32)...]
where the time goes in v4:
time: 91.5 us; the launch traced here: 91.3 us
  Pallas kernels  89.7 us (98%)
  local copies, waits for them, and re-layouts  1.57 us (2%)
    pallas_call x1, Pallas kernels, body(): pl.pallas_call(kernel, out_shape=jax.ShapeDtypeStruct((WIDTH, NODE), f32)...  89.7 us

profile of v4, /device:TPU:1, one launch (start us, length us, event | category | flops | bytes accessed | tf_op | source)
XLA Modules:
  0.0 91.3 jit_solution(15988037871140656021)
XLA Ops:
  0.0 89.7 %subspace_step.1 = f32[64,512]{1,0:T(8,128)} custom-call(f32[64,512]{1,0:T(8,128)} %initial.1, f32[1,512,512]{2,1,0:T(8,128)} %matrices.1, s32[1,512]{1,0:T(1,128)} %cmap_ref.1, s32[1,64]{1,0:T(1,128)} %low_ref.1, s32[1,64]{1,0:T(1,128)} %high_ref.1), custom_call_target="tpu_custom_call" | custom-call | tf_op jit(solution)/shard_map/subspace_step/pallas_call | solution.py:468
  89.7 1.6 %copy.7 = f32[64,512]{1,0:T(8,128)} copy(f32[64,512]{1,0:T(8,128)} %subspace_step.1) | data formatting | bytes 262144

commit v5 on v4

--- a/solution.py
+++ b/solution.py
@@ -218,11 +218,6 @@
         main = dot(jnp.concatenate([hi, lo], axis=0), ah[rows, first:last])
         return main[:WIDTH] + (main[WIDTH:] + dot(hi, al[rows, first:last]))
 
-    def ahead():
-        image[...] = apply(cur[:, RIM:], RIM, NODE, 0, NODE)
-
-    block_out[...] = ah[:RIM, :RIM].astype(f32) + al[:RIM, :RIM].astype(f32)
-
     def neighbour_copy(source, target, send, recv, slot, way, distance):
         to = lax.rem(c + (distance if way == 1 else cells - distance), cells)
         return pltpu.make_async_remote_copy(
@@ -231,9 +226,7 @@
         )
 
     blocks = [neighbour_copy(block_out, block_in.at[w], bs, br, 0, w, 1) for w in (0, 1)]
-    for copy in blocks:
-        copy.start()
-    ahead()
+    image[:, :RIM] = apply(cur[:, RIM:], RIM, NODE, 0, RIM)
     start.wait()
     got = rbuf[0, 1]
     first_rim = cur[:, :RIM]
@@ -250,10 +243,13 @@
         up_copy = halo_copy(slot, 1)
         down_copy.start()
         up_copy.start()
+        block_out[...] = ah[:RIM, :RIM].astype(f32) + al[:RIM, :RIM].astype(f32)
+        for copy in blocks:
+            copy.start()
         greeted(0)
         greet(1)
         factor = 1.0
-        inner = image[:, RIM:] + apply(now, 0, RIM, RIM, NODE)
+        inner = apply(cur[:, RIM:], RIM, NODE, RIM, NODE) + apply(now, 0, RIM, RIM, NODE)
         core = cur[:, RIM:]
         following = factor * (inner - center_value * core) / half_width - prev[:, RIM:]
         prev[:, RIM:] = core

time: 91.5 us -> 92.1 us (level)
  no operation moved by 1% of the time
where the time goes in v5:
time: 92.1 us; the launch traced here: 91.9 us
  Pallas kernels  90.3 us (98%)
  local copies, waits for them, and re-layouts  1.57 us (2%)
    pallas_call x1, Pallas kernels, body(): pl.pallas_call(kernel, out_shape=jax.ShapeDtypeStruct((WIDTH, NODE), f32)...  90.3 us

profile of v5, /device:TPU:1, one launch (start us, length us, event | category | flops | bytes accessed | tf_op | source)
XLA Modules:
  0.0 91.9 jit_solution(17726213590067839298)
XLA Ops:
  0.0 90.3 %subspace_step.1 = f32[64,512]{1,0:T(8,128)} custom-call(f32[64,512]{1,0:T(8,128)} %initial.1, f32[1,512,512]{2,1,0:T(8,128)} %matrices.1, s32[1,512]{1,0:T(1,128)} %cmap_ref.1, s32[1,64]{1,0:T(1,128)} %low_ref.1, s32[1,64]{1,0:T(1,128)} %high_ref.1), custom_call_target="tpu_custom_call" | custom-call | tf_op jit(solution)/shard_map/subspace_step/pallas_call | solution.py:464
  90.3 1.6 %copy.7 = f32[64,512]{1,0:T(8,128)} copy(f32[64,512]{1,0:T(8,128)} %subspace_step.1) | data formatting | bytes 262144
